TPU v7x, 32 devices: a whole 2x2x4 slice. The times are simulated.
32 devices in a mesh: dp: 4 (over z), latent: 8 (over y, x, core).
Axes of the slice: x: 2, y: 2, z: 4, core: 2. Of those that a mesh axis runs over, the one named last changes fastest.
Arguments:
- inputs: bfloat16 [64, 2048], P(('dp', 'latent')), may hold values from -6 to 6
- blocks: int32 [64, 4], P(('dp', 'latent')), may hold values from 0 to 127, all different within a row; in each aligned block of 16 rows (0 to 15, 16 to 31, ...) at most 2 rows name the same one
- weights: bfloat16 [8192, 2048], P('latent'), as said below
- enc_bias: float32 [8192], P('latent'), may hold values from -3 to 3
- dec_bias: float32 [2048], replicated, may hold values from -3 to 3
Outputs:
- recon: bfloat16 [64, 2048], P(('dp', 'latent'))
- grad_weights: float32 [8192, 2048], P('latent', 'dp')
- block_scores: float32 [128, 64], P('latent', 'dp')
Inputs may be any that keep to these rules, and one draw needn't show every extreme that they name: Each row names 4 different blocks. Within the rows of one data group (aligned runs of 16 rows) no block is named by more than 2 rows, and some block is named by exactly 2 rows. `weights`: rows have different lengths.
All inputs are finite; a program needn't handle non-finite values.
Results may differ from a plain program's by a relative error of at most 0.0068.
Values may be sent and summed in bfloat16 or wider, within the bound.
No kernel may reach another device: no remote copies, remote signals or barrier semaphores. Data moves between devices by JAX's collectives and lax.ppermute only.
A program may use at most 64 MiB of HBM per device.

v0:
```python
import jax
import jax.numpy as jnp
from jax import lax
from jax.sharding import PartitionSpec as P

BLK = 64
CAP = 2


def local(inputs, blocks, weights, enc_bias, dec_bias):
    lat_rows, width = weights.shape
    block_count = lat_rows // BLK
    centered = (inputs.astype(jnp.float32) - dec_bias).astype(jnp.bfloat16)
    panels, row_lists = (
        lax.all_gather(centered, "latent", axis=0, tiled=True),
        lax.all_gather(blocks, "latent", axis=0, tiled=True),
    )
    rows_group = panels.shape[0]
    squares = jnp.sum(jnp.square(weights.astype(jnp.float32)), axis=1)
    row_norms = jnp.sqrt(squares + 1e-06)
    unit_rows = (weights.astype(jnp.float32) / row_norms[:, None]).astype(jnp.bfloat16)
    unit_blocks = unit_rows.reshape(block_count, BLK, width)
    first_block = lax.axis_index("latent") * block_count
    block_ids = first_block + jnp.arange(block_count, dtype=jnp.int32)
    hit_rows = jnp.any(row_lists[None, :, :] == block_ids[:, None, None], axis=2).astype(jnp.int32)
    before = jnp.cumsum(hit_rows, axis=1) - hit_rows
    slot_ids = jnp.arange(CAP, dtype=jnp.int32)
    picked = (hit_rows[:, None, :] == 1) & (before[:, None, :] == slot_ids[None, :, None])
    row_ids = jnp.sum(
        jnp.where(picked, jnp.arange(rows_group, dtype=jnp.int32)[None, None, :], 0), axis=2
    )
    live_slots = jnp.any(picked, axis=2).astype(jnp.float32)[:, :, None]
    full_dot = jnp.dot(unit_rows, panels.T, preferred_element_type=jnp.float32)
    block_scores = jnp.mean(
        jax.nn.softplus(full_dot + enc_bias[:, None]).reshape(block_count, BLK, rows_group), axis=1
    )
    dot_blocks = full_dot.reshape(block_count, BLK, rows_group)
    base_pre = jnp.transpose(
        jnp.take_along_axis(
            dot_blocks, jnp.broadcast_to(row_ids[:, None, :], (block_count, BLK, CAP)), axis=2
        ),
        (0, 2, 1),
    )
    preact = base_pre + enc_bias.reshape(block_count, BLK)[:, None, :]
    latent_codes = (jax.nn.softplus(preact) * live_slots).astype(jnp.bfloat16)
    slot_rows = panels[row_ids]
    contrib = jnp.einsum(
        "jcm,jmd->jcd", latent_codes, unit_blocks, preferred_element_type=jnp.float32
    )
    partial_value = (
        jnp.zeros((rows_group, width), jnp.float32)
        .at[row_ids.reshape(-1)]
        .add(contrib.reshape(-1, width))
    )
    own_sums = lax.psum_scatter(partial_value, "latent", scatter_dimension=0, tiled=True)
    recon_full = dec_bias + own_sums
    recon_rows = recon_full.astype(jnp.bfloat16)
    errors = (recon_full - inputs.astype(jnp.float32)).astype(jnp.bfloat16)
    all_errors = lax.all_gather(errors, "latent", axis=0, tiled=True)
    slot_errors = all_errors[row_ids]
    code_grad = jnp.einsum(
        "jcd,jmd->jcm", slot_errors, unit_blocks, preferred_element_type=jnp.float32
    )
    pre_grad = (code_grad * jax.nn.sigmoid(preact) * live_slots).astype(jnp.bfloat16)
    along_unit = jnp.sum(
        latent_codes.astype(jnp.float32) * code_grad + pre_grad.astype(jnp.float32) * base_pre,
        axis=1,
    )
    norm_blocks = row_norms.reshape(block_count, BLK)
    groups = lax.axis_size("dp")
    col_count = width // groups
    moved_rows, moved_errors = (
        lax.all_to_all(slot_rows[None], "dp", split_axis=3, concat_axis=0, tiled=True),
        lax.all_to_all(slot_errors[None], "dp", split_axis=3, concat_axis=0, tiled=True),
    )
    got_codes, got_grad = (
        lax.all_gather(latent_codes[None], "dp", axis=0, tiled=True),
        lax.all_gather(pre_grad[None], "dp", axis=0, tiled=True),
    )
    got_along = lax.all_gather(along_unit[None], "dp", axis=0, tiled=True)
    col_start = lax.axis_index("dp") * col_count
    unit_cols = (
        lax.dynamic_slice_in_dim(unit_rows, col_start, col_count, 1)
        .astype(jnp.float32)
        .reshape(block_count, BLK, col_count)
    )
    got_left = jnp.concatenate([got_codes, got_grad], axis=2)
    got_right = jnp.concatenate([moved_errors, moved_rows], axis=2)
    outer_terms = jnp.einsum(
        "gjcm,gjcd->gjmd", got_left, got_right, preferred_element_type=jnp.float32
    )
    group_parts = (outer_terms - unit_cols[None] * got_along[..., None]) / norm_blocks[
        None, :, :, None
    ]
    group_parts = lax.optimization_barrier(group_parts.astype(jnp.bfloat16)).astype(jnp.float32)
    grad_weights = jnp.sum(group_parts, axis=0).reshape(lat_rows, col_count)
    return (recon_rows, grad_weights, block_scores)


def solution(mesh):
    in_specs = (
        P(("dp", "latent"), None),
        P(("dp", "latent"), None),
        P("latent", None),
        P("latent"),
        P(),
    )
    out_specs = (P(("dp", "latent"), None), P("latent", "dp"), P("latent", "dp"))
    return jax.shard_map(local, mesh=mesh, in_specs=in_specs, out_specs=out_specs, check_vma=False)
```

profile of v0, /device:TPU:0, one launch (start us, length us, event | category | flops | bytes accessed | tf_op | source)
XLA Modules:
  0.0 189.1 jit_solution(11037067307001685502)
XLA Ops:
  7.2 10.5 %all-gather.3 = s32[8,2,4]{2,1,0:T(2,128)S(1)} all-gather(s32[1,2,4]{2,1,0:T(2,128)} %bitcast.63), channel_id=1, replica_groups=mesh['dp'=4,'latent'=8] {'latent'}, dimensions={0}, use_global_device_ids=true | all-gather | bytes 288 | tf_op jit(solution)/shard_map/all_gather | solution.py:16
  17.7 0.1 copy.63
  17.7 0.1 compare_reduce_fusion
  17.8 0.2 reduce_window_sum.11
  18.0 0.1 select_reduce_fusion
  18.1 0.1 copy.71
  18.2 0.1 reshape.126
  18.3 0.7 fusion.17
  19.1 9.1 %all-gather.4 = bf16[8,2,2048]{2,1,0:T(2,128)(2,1)S(1)} all-gather(bf16[1,2,2048]{2,1,0:T(2,128)(2,1)S(1)} %fusion.17), channel_id=1, replica_groups=mesh['dp'=4,'latent'=8] {'latent'}, dimensions={0}, use_global_device_ids=true | all-gather | bytes 73728 | tf_op jit(solution)/shard_map/all_gather | solution.py:15
  28.2 0.0 copy-start.2
  28.2 0.7 gather_fusion.1
  28.9 0.1 broadcast_in_dim.78
  29.0 0.8 copy.75
  29.7 1.7 reshape.170
  31.5 4.9 %all-to-all-start.1 = ((bf16[4,2,8192]{2,1,0:T(2,128)(2,1)}), bf16[4,2,8192]{2,1,0:T(2,128)(2,1)}, u32[]{:S(2)}, u32[]{:S(2)}) async-start(bf16[4,2,8192]{2,1,0:T(2,128)(2,1)} %reshape.170), calls=%async_computation.1 | async-start | bytes 262144 | tf_op jit(solution)/shard_map/all_to_all | solution.py:73
  36.3 0.1 fusion.15
  36.5 0.1 copy.64
  36.6 0.7 copy.65
  37.2 0.7 copy.66
  37.9 0.1 shift-left_or_fusion
  38.0 3.1 %fusion = f32[1024]{0:T(1024)S(1)} fusion(bf16[1024,2048]{1,0:T(8,128)(2,1)} %param.7), kind=kLoop, calls=%fused_computation.6 | loop fusion | flops 6290432 | bytes 4198400 | tf_op jit(solution)/shard_map/reduce_sum | solution.py:19
  41.1 0.7 add.114
  41.8 0.7 copy.70
  42.5 0.1 reshape.117
  42.5 0.6 fusion.19
  43.1 0.2 copy.68
  43.3 0.3 reshape.140
  43.6 3.9 %fusion.1 = bf16[1024,2048]{1,0:T(8,128)(2,1)S(1)} fusion(bf16[1024,2048]{1,0:T(8,128)(2,1)} %param.7, f32[1024]{0:T(1024)S(1)} %add_sqrt_fusion), kind=kLoop, calls=%fused_computation.7 | loop fusion | flops 6291456 | bytes 8392704 | tf_op jit(solution)/shard_map/convert_element_type | solution.py:21
  47.5 2.0 %compare_select_fusion = (f32[1024,16]{0,1:T(8,128)}, f32[1024,16]{0,1:T(8,128)S(1)}) fusion(f32[1024]{0:T(1024)S(1)} %copy-done.2, bf16[1024,2048]{1,0:T(8,128)(2,1)S(1)} %fusion.1, bf16[16,2048]{1,0:T(8,128)(2,1)S(1)} %reshape.164), kind=kOutput, calls=%fused_computation.13 | convolution fusion | flops 67223552 | bytes 4395008 | tf_op jit(solution)/shard_map/dot_general | solution.py:33
  49.5 0.1 reshape.118
  49.6 16.8 %gather_fusion.2 = f32[2048]{0:T(1024)S(1)} fusion(f32[16,64,16]{1,0,2:T(8,128)S(1)} %reshape.118, s32[2048]{0:T(1024)S(1)} %reshape.140), kind=kCustom, calls=%fused_computation.2 | custom fusion | bytes 40960 | tf_op jit(solution)/shard_map/jit(take_along_axis)/gather | solution.py:39
  66.5 0.5 reshape.143
  67.0 0.2 copy.69
  67.2 0.1 fusion.13
  67.4 2.8 %fusion.21 = f32[16,2,2048]{2,1,0:T(2,128)S(1)} fusion(bf16[16,2,64]{2,1,0:T(2,128)(2,1)S(1)} %get-tuple-element.14, bf16[16,64,2048]{2,1,0:T(8,128)(2,1)} %bitcast.49), kind=kOutput, calls=%fused_computation.53 | convolution fusion | flops 8388608 | bytes 4460544 | tf_op jit(solution)/shard_map/jcm,jmd->jcd/dot_general | solution.py:47
  70.2 0.2 reshape.150
  70.4 1.7 scatter_custom_fusion
  72.1 0.0 all-reduce.3.cloned.1.call-update
  72.2 0.1 reshape.122
  72.3 0.1 reduce_sum.52
  72.4 1.3 constant_dynamic-slice_fusion
  73.7 0.1 sqrt.15
  73.8 0.7 copy.78
  74.4 0.3 convert.1
  74.7 0.6 dynamic-slice
  76.0 13.7 %all-gather = bf16[64,2,64]{2,1,0:T(2,128)(2,1)S(1)} all-gather(bf16[16,2,64]{2,1,0:T(2,128)(2,1)S(1)} %get-tuple-element.14), channel_id=2, replica_groups=mesh['dp'=4,'latent'=8] {'dp'}, dimensions={0}, use_global_device_ids=true | all-gather | bytes 20480 | tf_op jit(solution)/shard_map/all_gather | solution.py:77
  89.7 36.1 %all-reduce.3.cloned.1.call-done = f32[16,2048]{1,0:T(8,128)} async-done(((f32[16,2048]{1,0:T(8,128)}), f32[16,2048]{1,0:T(8,128)}) %all-reduce.3.cloned.1.call-update) | async-done | bytes 131088
  125.7 1.5 fusion.18
  127.2 8.7 %all-gather.5 = bf16[8,2,2048]{2,1,0:T(2,128)(2,1)S(1)} all-gather(bf16[1,2,2048]{2,1,0:T(2,128)(2,1)S(1)} %get-tuple-element.16), channel_id=1, replica_groups=mesh['dp'=4,'latent'=8] {'latent'}, dimensions={0}, use_global_device_ids=true | all-gather | bytes 73728 | tf_op jit(solution)/shard_map/all_gather | solution.py:59
  136.0 0.7 gather_fusion
  136.6 0.1 broadcast_in_dim.77
  136.7 0.1 reshape.125
  136.8 0.8 copy.72
  137.6 1.7 reshape.172
  139.3 4.6 %all-to-all-start = ((bf16[4,2,8192]{2,1,0:T(2,128)(2,1)}), bf16[4,2,8192]{2,1,0:T(2,128)(2,1)S(1)}, u32[]{:S(2)}, u32[]{:S(2)}) async-start(bf16[4,2,8192]{2,1,0:T(2,128)(2,1)} %reshape.172), calls=%async_computation | async-start | bytes 262144 | tf_op jit(solution)/shard_map/all_to_all | solution.py:74
  143.9 3.4 %add_reduce_fusion = (f32[16,64]{1,0:T(8,128)S(1)}, bf16[16,2,64]{2,1,0:T(2,128)(2,1)S(1)}) fusion(f32[16,2,64]{2,1,0:T(2,128)S(1)} %get-tuple-element.15, bf16[16,2,64]{2,1,0:T(2,128)(2,1)S(1)} %get-tuple-element.14, f32[16,2]{1,0:T(8,128)S(1)} %copy-done.12, f32[16,64]{1,0:T(8,128)S(1)} %copy-done.11, bf16[16,2,2048]{2,1,0:T(2,128)(2,1)S(1)} %reshape.125, ...), kind=kOutput, calls=%fused_computation.31 | convolution fusion | flops 8414208 | bytes 4350080 | tf_op jit(solution)/shard_map/jcd,jmd->jcm/dot_general | solution.py:61
  147.3 13.7 %all-gather.2 = f32[64,64]{1,0:T(8,128)S(1)} all-gather(f32[16,64]{1,0:T(8,128)S(1)} %get-tuple-element.12), channel_id=4, replica_groups=mesh['dp'=4,'latent'=8] {'dp'}, dimensions={0}, use_global_device_ids=true | all-gather | bytes 20480 | tf_op jit(solution)/shard_map/all_gather | solution.py:80
  161.0 13.1 %all-gather.1 = bf16[64,2,64]{2,1,0:T(2,128)(2,1)S(1)} all-gather(bf16[16,2,64]{2,1,0:T(2,128)(2,1)S(1)} %get-tuple-element.13), channel_id=3, replica_groups=mesh['dp'=4,'latent'=8] {'dp'}, dimensions={0}, use_global_device_ids=true | all-gather | bytes 20480 | tf_op jit(solution)/shard_map/all_gather | solution.py:78
  174.1 1.6 reshape.171
  175.8 0.7 copy.77
  176.5 0.7 reshape.173
  177.2 0.7 copy.74
  178.0 2.1 %divide_convert_fusion = bf16[4,16,64,512]{3,2,1,0:T(8,128)(2,1)S(1)} fusion(f32[16,64]{1,0:T(8,128)S(1)} %sqrt.15, f32[4,16,64]{2,1,0:T(8,128)S(1)} %bitcast.60, f32[16,64,512]{2,1,0:T(8,128)S(1)} %convert.1, bf16[4,16,2,512]{3,2,1,0:T(2,128)(2,1)S(1)} %bitcast.57, bf16[4,16,2,512]{3,2,1,0:T(2,128)(2,1)S(1)} %bitcast.58, ...), kind=kOutput, calls=%fused_computation.9 | convolution fusion | flops 25755648 | bytes 6606848 | tf_op jit(solution)/shard_map/gjcm,gjcd->gjmd/dot_general | solution.py:89
  180.1 2.1 %convert_reduce_fusion = f32[16,64,512]{2,1,0:T(8,128)} fusion(bf16[4,16,64,512]{3,2,1,0:T(8,128)(2,1)S(1)} %divide_convert_fusion), kind=kLoop, calls=%fused_computation.8 | loop fusion | flops 3670016 | bytes 6291456 | tf_op jit(solution)/shard_map/reduce_sum | solution.py:96
  (46 shorter events, 0.2 us)
Async XLA Ops:
  18.3 10.5 %copy-start.3 = (s32[1024]{0:T(1024)}, s32[1024]{0:T(1024)S(1)}, u32[]{:S(2)}) copy-start(s32[1024]{0:T(1024)S(1)} %pad_clamp_fusion) | copy-start | bytes 12292
  28.2 12.9 %copy-start.2 = (f32[1024]{0:T(1024)S(1)}, f32[1024]{0:T(1024)}, u32[]{:S(2)}) copy-start(f32[1024]{0:T(1024)} %param.8) | copy-start | bytes 12292
  31.5 107.9 %all-to-all-start.1 = ((bf16[4,2,8192]{2,1,0:T(2,128)(2,1)}), bf16[4,2,8192]{2,1,0:T(2,128)(2,1)}, u32[]{:S(2)}, u32[]{:S(2)}) async-start(bf16[4,2,8192]{2,1,0:T(2,128)(2,1)} %reshape.170), calls=%async_computation.1 | async-start | bytes 262144 | tf_op jit(solution)/shard_map/all_to_all | solution.py:73
  36.3 89.4 %all-reduce.3.cloned.1.call-start = ((), (), s32[]{:S(2)}) async-start(), calls=%async_computation.2 | async-start | bytes 262144
  36.6 6.5 %copy-start.5 = (s32[16,2]{1,0:T(8,128)}, s32[16,2]{1,0:T(8,128)S(1)}, u32[]{:S(2)}) copy-start(s32[16,2]{1,0:T(8,128)S(1)} %copy.64) | copy-start | bytes 388
  41.1 6.4 %copy-start.7 = (f32[1024]{0:T(1024)}, f32[1024]{0:T(1024)S(1)}, u32[]{:S(2)}) copy-start(f32[1024]{0:T(1024)S(1)} %add_sqrt_fusion) | copy-start | bytes 12292
  47.5 2.0 %copy-start = (bf16[1024,2048]{1,0:T(8,128)(2,1)}, bf16[1024,2048]{1,0:T(8,128)(2,1)S(1)}, u32[]{:S(2)}) copy-start(bf16[1024,2048]{1,0:T(8,128)(2,1)S(1)} %fusion.1) | copy-start | bytes 12582916
  49.6 17.6 %copy-start.6 = (s32[16,2]{1,0:T(8,128)S(1)}, s32[16,2]{1,0:T(8,128)}, u32[]{:S(2)}) copy-start(s32[16,2]{1,0:T(8,128)} %copy-done.5) | copy-start | bytes 388
  49.6 17.6 %copy-start.11 = (f32[16,64]{1,0:T(8,128)S(1)}, f32[16,64]{1,0:T(8,128)}, u32[]{:S(2)}) copy-start(f32[16,64]{1,0:T(8,128)} %add.114) | copy-start | bytes 12292
  49.6 17.6 %copy-start.12 = (f32[16,2]{1,0:T(8,128)S(1)}, f32[16,2]{1,0:T(8,128)}, u32[]{:S(2)}) copy-start(f32[16,2]{1,0:T(8,128)} %copy.70) | copy-start | bytes 388
  49.6 17.6 %copy-start.13 = (s32[16,2]{1,0:T(8,128)S(1)}, s32[16,2]{1,0:T(8,128)}, u32[]{:S(2)}) copy-start(s32[16,2]{1,0:T(8,128)} %copy.66) | copy-start | bytes 388
  49.6 17.6 %copy-start.14 = (pred[16,2]{1,0:T(8,128)(4,1)S(1)}, pred[16,2]{1,0:T(8,128)(4,1)}, u32[]{:S(2)}) copy-start(pred[16,2]{1,0:T(8,128)(4,1)} %copy.65) | copy-start | bytes 100
  66.5 5.7 %copy-start.1 = (f32[1024,16]{0,1:T(8,128)S(1)}, f32[1024,16]{0,1:T(8,128)}, u32[]{:S(2)}) copy-start(f32[1024,16]{0,1:T(8,128)} %get-tuple-element.20) | copy-start | bytes 196612
  66.9 6.8 %copy-start.8 = (f32[1024]{0:T(1024)S(1)}, f32[1024]{0:T(1024)}, u32[]{:S(2)}) copy-start(f32[1024]{0:T(1024)} %copy-done.7) | copy-start | bytes 12292
  70.2 4.5 %copy-start.15 = (u32[32]{0:T(128)S(1)}, u32[32]{0:T(128)}, u32[]{:S(2)}) copy-start(u32[32]{0:T(128)} %constant.78) | copy-start | bytes 388
  70.2 55.5 %copy-start.9 = (bf16[2,2048]{1,0:T(2,128)(2,1)S(1)}, bf16[2,2048]{1,0:T(2,128)(2,1)}, u32[]{:S(2)}) copy-start(bf16[2,2048]{1,0:T(2,128)(2,1)} %param.5) | copy-start | bytes 24580
  70.2 55.5 %copy-start.10 = (f32[2048]{0:T(1024)S(1)}, f32[2048]{0:T(1024)}, u32[]{:S(2)}) copy-start(f32[2048]{0:T(1024)} %param.9) | copy-start | bytes 24580
  70.2 65.7 %copy-start.4 = (s32[1024]{0:T(1024)S(1)}, s32[1024]{0:T(1024)}, u32[]{:S(2)}) copy-start(s32[1024]{0:T(1024)} %copy-done.3) | copy-start | bytes 12292
  139.3 37.2 %all-to-all-start = ((bf16[4,2,8192]{2,1,0:T(2,128)(2,1)}), bf16[4,2,8192]{2,1,0:T(2,128)(2,1)S(1)}, u32[]{:S(2)}, u32[]{:S(2)}) async-start(bf16[4,2,8192]{2,1,0:T(2,128)(2,1)} %reshape.172), calls=%async_computation | async-start | bytes 262144 | tf_op jit(solution)/shard_map/all_to_all | solution.py:74
Sparse Core Ops, SparseCore 0:
  72.3 53.3 all-reduce.2
where the time goes:
time: 190 us; the launch traced here: 189 us
  blocking collectives  68.8 us (36%)
  waiting for transfers between devices  36.1 us (19%)
  local copies, waits for them, and re-layouts  34.6 us (18%)
  between operations  15.1 us (8%)
  other arithmetic  14.7 us (8%)
  matrix products  10.3 us (5%)
  starting transfers between devices  9.47 us (5%)
    unnamed x2, waiting for transfers between devices  36.1 us
    gather x5, local copies, waits for them, and re-layouts, local(): jnp.take_along_axis(dot_blocks, jnp.broadcast_to(row_ids[:, None, :], (bl...  18 us
    all_gather x1, blocking collectives, local(): got_along = lax.all_gather(along_unit[None], 'dp', axis=0, tiled=True)  13.7 us
    all_gather x1, blocking collectives, local(): lax.all_gather(latent_codes[None], 'dp', axis=0, tiled=True)  13.7 us
    all_gather x1, blocking collectives, local(): lax.all_gather(pre_grad[None], 'dp', axis=0, tiled=True)  13.1 us
    all_gather x1, blocking collectives, local(): lax.all_gather(blocks, 'latent', axis=0, tiled=True)  10.5 us
    all_gather x1, blocking collectives, local(): lax.all_gather(centered, 'latent', axis=0, tiled=True)  9.08 us
    all_gather x1, blocking collectives, local(): all_errors = lax.all_gather(errors, 'latent', axis=0, tiled=True)  8.72 us
  transfers between devices with their start and end apart: 3, of which 1 were waited for; matrix products, arithmetic and copies ran while one was open for 26% of the time, Pallas kernels for 0%

commit v1 on v0

--- a/solution.py
+++ b/solution.py
@@ -1,10 +1,34 @@
+import functools
 import jax
 import jax.numpy as jnp
 from jax import lax
 from jax.sharding import PartitionSpec as P
+from jax.lax import axis_index, axis_size, ppermute
 
 BLK = 64
 CAP = 2
+
+
+def _save_members_all(frame_in, dev_axis):
+    z_new, w1, left_arr = (axis_size(dev_axis), axis_index(dev_axis), frame_in.shape[0])
+    f_next, spare = (frame_in, 1)
+    while spare < z_new:
+        f_next = jnp.concatenate(
+            [
+                f_next,
+                ppermute(
+                    f_next,
+                    dev_axis,
+                    tuple(((tick, (tick - spare) % z_new) for tick in range(z_new))),
+                ),
+            ],
+            axis=0,
+        )
+        spare = 2 * spare
+    return jnp.roll(f_next, shift=w1 * left_arr, axis=0)
+
+
+frame_push = functools.partial(_save_members_all, dev_axis="dp")
 
 
 def local(inputs, blocks, weights, enc_bias, dec_bias):
@@ -75,7 +99,7 @@
     )
     got_codes, got_grad = (
         lax.all_gather(latent_codes[None], "dp", axis=0, tiled=True),
-        lax.all_gather(pre_grad[None], "dp", axis=0, tiled=True),
+        frame_push(pre_grad[None]),
     )
     got_along = lax.all_gather(along_unit[None], "dp", axis=0, tiled=True)
     col_start = lax.axis_index("dp") * col_count

time: 190 us -> 187 us (0.984)
  blocking collectives: 68.8 us -> 54.9 us
  waiting for transfers between devices: 36.1 us -> 43.6 us
  starting transfers between devices: 9.47 us -> 12.4 us
    all_gather x1 -> x0, blocking collectives: 13.1 us -> none  [local(): lax.all_gather(pre_grad[None], 'dp', axis=0, tiled=True)]
    ppermute x0 -> x2, starting transfers between devices: none -> 4.2 us  [_save_members_all(): ppermute(f_next, dev_axis, tuple(((tick, (tick - spare) % z_new) for tick...]
    ppermute x0 -> x2, waiting for transfers between devices: none -> 4.05 us  [_save_members_all(): ppermute(f_next, dev_axis, tuple(((tick, (tick - spare) % z_new) for tick...]
    all_to_all x1, waiting for transfers between devices: 0.01 us -> 3.45 us  [local(): lax.all_to_all(slot_errors[None], 'dp', split_axis=3, concat_axis=0, tile...]
    unnamed x41 -> x45, local copies, waits for them, and re-layouts: 7.23 us -> 7.3 us
  transfers between devices with their start and end apart: 3 -> 5, of which waited for: 1 -> 3; matrix products, arithmetic and copies ran while one was open for 26% -> 27% of each run, Pallas kernels for 0% -> 0%
where the time goes in v1:
time: 187 us; the launch traced here: 186 us
  blocking collectives  54.9 us (29%)
  waiting for transfers between devices  43.6 us (23%)
  local copies, waits for them, and re-layouts  34.7 us (19%)
  between operations  15.2 us (8%)
  other arithmetic  14.7 us (8%)
  starting transfers between devices  12.4 us (7%)
  matrix products  10.3 us (6%)
    unnamed x2, waiting for transfers between devices  36.1 us
    gather x5, local copies, waits for them, and re-layouts, local(): jnp.take_along_axis(dot_blocks, jnp.broadcast_to(row_ids[:, None, :], (bl...  18 us
    all_gather x1, blocking collectives, local(): lax.all_gather(latent_codes[None], 'dp', axis=0, tiled=True)  13.7 us
    all_gather x1, blocking collectives, local(): got_along = lax.all_gather(along_unit[None], 'dp', axis=0, tiled=True)  13.1 us
    all_gather x1, blocking collectives, local(): lax.all_gather(blocks, 'latent', axis=0, tiled=True)  10.5 us
    all_gather x1, blocking collectives, local(): lax.all_gather(centered, 'latent', axis=0, tiled=True)  9.08 us
    all_gather x1, blocking collectives, local(): all_errors = lax.all_gather(errors, 'latent', axis=0, tiled=True)  8.54 us
    unnamed x45, local copies, waits for them, and re-layouts  7.3 us
  transfers between devices with their start and end apart: 5, of which 3 were waited for; matrix products, arithmetic and copies ran while one was open for 27% of the time, Pallas kernels for 0%

profile of v1, /device:TPU:0, one launch (start us, length us, event | category | flops | bytes accessed | tf_op | source)
XLA Modules:
  0.0 185.8 jit_solution(11527382754691550173)
XLA Ops:
  7.2 10.5 %all-gather.2 = s32[8,2,4]{2,1,0:T(2,128)S(1)} all-gather(s32[1,2,4]{2,1,0:T(2,128)} %bitcast.66), channel_id=1, replica_groups=mesh['dp'=4,'latent'=8] {'latent'}, dimensions={0}, use_global_device_ids=true | all-gather | bytes 288 | tf_op jit(solution)/shard_map/all_gather | solution.py:40
  17.7 0.1 copy.63
  17.7 0.1 compare_reduce_fusion
  17.8 0.2 reduce_window_sum.11
  18.0 0.1 select_reduce_fusion
  18.1 0.1 copy.71
  18.2 0.1 reshape.126
  18.3 0.7 fusion.17
  19.1 9.1 %all-gather.3 = bf16[8,2,2048]{2,1,0:T(2,128)(2,1)S(1)} all-gather(bf16[1,2,2048]{2,1,0:T(2,128)(2,1)S(1)} %fusion.17), channel_id=1, replica_groups=mesh['dp'=4,'latent'=8] {'latent'}, dimensions={0}, use_global_device_ids=true | all-gather | bytes 73728 | tf_op jit(solution)/shard_map/all_gather | solution.py:39
  28.2 0.7 gather_fusion.1
  28.9 0.1 broadcast_in_dim.78
  29.0 0.8 copy.75
  29.7 1.7 reshape.169
  31.5 4.9 %all-to-all-start.1 = ((bf16[4,2,8192]{2,1,0:T(2,128)(2,1)}), bf16[4,2,8192]{2,1,0:T(2,128)(2,1)}, u32[]{:S(2)}, u32[]{:S(2)}) async-start(bf16[4,2,8192]{2,1,0:T(2,128)(2,1)} %reshape.169), calls=%async_computation.1 | async-start | bytes 262144 | tf_op jit(solution)/shard_map/all_to_all | solution.py:97
  36.3 0.1 fusion.15
  36.5 0.1 copy.64
  36.6 0.7 copy.65
  37.2 0.7 copy.66
  37.9 0.1 shift-left_or_fusion
  38.0 3.1 %fusion = f32[1024]{0:T(1024)S(1)} fusion(bf16[1024,2048]{1,0:T(8,128)(2,1)} %param.7), kind=kLoop, calls=%fused_computation.6 | loop fusion | flops 6290432 | bytes 4198400 | tf_op jit(solution)/shard_map/reduce_sum | solution.py:43
  41.1 0.7 add.124
  41.8 0.7 copy.70
  42.5 0.1 reshape.117
  42.5 0.5 fusion.19
  43.1 0.2 copy.68
  43.3 0.3 reshape.140
  43.6 3.9 %fusion.1 = bf16[1024,2048]{1,0:T(8,128)(2,1)S(1)} fusion(bf16[1024,2048]{1,0:T(8,128)(2,1)} %param.7, f32[1024]{0:T(1024)S(1)} %add_sqrt_fusion), kind=kLoop, calls=%fused_computation.7 | loop fusion | flops 6291456 | bytes 8392704 | tf_op jit(solution)/shard_map/convert_element_type | solution.py:45
  47.5 2.0 %compare_select_fusion = (f32[1024,16]{0,1:T(8,128)}, f32[1024,16]{0,1:T(8,128)S(1)}) fusion(f32[1024]{0:T(1024)S(1)} %copy-done.2, bf16[1024,2048]{1,0:T(8,128)(2,1)S(1)} %fusion.1, bf16[16,2048]{1,0:T(8,128)(2,1)S(1)} %reshape.163), kind=kOutput, calls=%fused_computation.13 | convolution fusion | flops 67223552 | bytes 4395008 | tf_op jit(solution)/shard_map/dot_general | solution.py:57
  49.5 0.1 reshape.118
  49.6 16.8 %gather_fusion.2 = f32[2048]{0:T(1024)S(1)} fusion(f32[16,64,16]{1,0,2:T(8,128)S(1)} %reshape.118, s32[2048]{0:T(1024)S(1)} %reshape.140), kind=kCustom, calls=%fused_computation.2 | custom fusion | bytes 40960 | tf_op jit(solution)/shard_map/jit(take_along_axis)/gather | solution.py:63
  66.5 0.5 reshape.143
  67.0 0.2 copy.69
  67.2 0.1 fusion.13
  67.4 2.8 %fusion.21 = f32[16,2,2048]{2,1,0:T(2,128)S(1)} fusion(bf16[16,2,64]{2,1,0:T(2,128)(2,1)S(1)} %get-tuple-element.14, bf16[16,64,2048]{2,1,0:T(8,128)(2,1)} %bitcast.51), kind=kOutput, calls=%fused_computation.61 | convolution fusion | flops 8388608 | bytes 4460544 | tf_op jit(solution)/shard_map/jcm,jmd->jcd/dot_general | solution.py:71
  70.2 0.2 reshape.150
  70.4 1.7 scatter_custom_fusion
  72.2 0.1 reshape.122
  72.3 0.1 reduce_sum.52
  72.4 1.3 constant_dynamic-slice_fusion
  73.8 0.7 copy.78
  74.5 0.3 convert.1
  74.8 0.6 dynamic-slice
  76.0 13.7 %all-gather = bf16[64,2,64]{2,1,0:T(2,128)(2,1)S(1)} all-gather(bf16[16,2,64]{2,1,0:T(2,128)(2,1)S(1)} %get-tuple-element.14), channel_id=2, replica_groups=mesh['dp'=4,'latent'=8] {'dp'}, dimensions={0}, use_global_device_ids=true | all-gather | bytes 20480 | tf_op jit(solution)/shard_map/all_gather | solution.py:101
  89.7 36.1 %all-reduce.3.cloned.1.call-done = f32[16,2048]{1,0:T(8,128)} async-done(((f32[16,2048]{1,0:T(8,128)}), f32[16,2048]{1,0:T(8,128)}) %all-reduce.3.cloned.1.call-update) | async-done | bytes 131088
  125.7 1.5 fusion.18
  127.2 8.5 %all-gather.4 = bf16[8,2,2048]{2,1,0:T(2,128)(2,1)S(1)} all-gather(bf16[1,2,2048]{2,1,0:T(2,128)(2,1)S(1)} %get-tuple-element.16), channel_id=1, replica_groups=mesh['dp'=4,'latent'=8] {'latent'}, dimensions={0}, use_global_device_ids=true | all-gather | bytes 73728 | tf_op jit(solution)/shard_map/all_gather | solution.py:83
  135.8 0.7 gather_fusion
  136.4 0.1 broadcast_in_dim.77
  136.5 0.1 reshape.125
  136.6 3.4 %constant_dynamic-update-slice_fusion.5 = (bf16[8,16,2,64]{3,2,1,0:T(2,128)(2,1)S(1)}, bf16[16,2,64]{2,1,0:T(2,128)(2,1)S(1)}, f32[16,2,64]{2,1,0:T(2,128)S(1)}) fusion(f32[16,2]{1,0:T(8,128)S(1)} %copy-done.12, f32[16,2,64]{2,1,0:T(2,128)S(1)} %get-tuple-element.15, f32[16,64]{1,0:T(8,128)S(1)} %copy-done.11, bf16[16,2,2048]{2,1,0:T(2,128)(2,1)S(1)} %reshape.125, ...), kind=kOutput, calls=%fused_computation.43 | convolution fusion | flops 8402943 | bytes 4370560 | tf_op jit(solution)/shard_map/jcd,jmd->jcm/dot_general | solution.py:85
  140.1 3.6 %collective-permute-start = (bf16[1,16,2,64]{3,2,1,0:T(2,128)(2,1)S(1)}, bf16[1,16,2,64]{3,2,1,0:T(2,128)(2,1)S(1)}, u32[]{:S(2)}, u32[]{:S(2)}) collective-permute-start(bf16[1,16,2,64]{3,2,1,0:T(2,128)(2,1)S(1)} %bitcast.61), channel_id=1, source_target_pairs={{0,24},{8,0},{16,8},{24,16},{1,25},{9,1},{17,9},{25,17},{2,26},{10... | collective-permute-start | bytes 12296 | tf_op jit(solution)/shard_map/ppermute | solution.py:19
  143.6 0.8 copy.72
  144.4 1.7 reshape.171
  146.1 13.1 %all-gather.1 = f32[64,64]{1,0:T(8,128)S(1)} all-gather(f32[16,64]{1,0:T(8,128)S(1)} %add_reduce_fusion), channel_id=3, replica_groups=mesh['dp'=4,'latent'=8] {'dp'}, dimensions={0}, use_global_device_ids=true | all-gather | bytes 20480 | tf_op jit(solution)/shard_map/all_gather | solution.py:104
  159.3 0.6 collective-permute-start.1
  159.9 4.0 %collective-permute-done.1 = bf16[2,16,2,64]{3,2,1,0:T(2,128)(2,1)S(1)} collective-permute-done((bf16[2,16,2,64]{3,2,1,0:T(2,128)(2,1)S(1)}, bf16[2,16,2,64]{3,2,1,0:T(2,128)(2,1)S(1)}, u32[]{:S(2)}, u32[]{:S(2)}) %collective-permute-start.1) | collective-permute-done | bytes 8224 | tf_op jit(solution)/shard_map/ppermute | solution.py:19
  164.1 3.3 %all-to-all-start = ((bf16[4,2,8192]{2,1,0:T(2,128)(2,1)}), bf16[4,2,8192]{2,1,0:T(2,128)(2,1)S(1)}, u32[]{:S(2)}, u32[]{:S(2)}) async-start(bf16[4,2,8192]{2,1,0:T(2,128)(2,1)} %reshape.171), calls=%async_computation | async-start | bytes 262144 | tf_op jit(solution)/shard_map/all_to_all | solution.py:98
  167.5 1.6 reshape.170
  169.1 0.7 copy.77
  169.8 3.4 %all-to-all-done = bf16[4,2,8192]{2,1,0:T(2,128)(2,1)S(1)} async-done(((bf16[4,2,8192]{2,1,0:T(2,128)(2,1)}), bf16[4,2,8192]{2,1,0:T(2,128)(2,1)S(1)}, u32[]{:S(2)}, u32[]{:S(2)}) %all-to-all-start) | async-done | bytes 131104 | tf_op jit(solution)/shard_map/all_to_all | solution.py:98
  173.3 0.7 reshape.172
  174.0 0.7 copy.74
  174.7 2.1 %divide_convert_fusion = bf16[4,16,64,512]{3,2,1,0:T(8,128)(2,1)S(1)} fusion(f32[16,64]{1,0:T(8,128)S(1)} %sqrt.15, f32[4,16,64]{2,1,0:T(8,128)S(1)} %bitcast.64, f32[16,64,512]{2,1,0:T(8,128)S(1)} %convert.1, bf16[4,16,2,512]{3,2,1,0:T(2,128)(2,1)S(1)} %bitcast.59, bf16[4,16,2,512]{3,2,1,0:T(2,128)(2,1)S(1)} %bitcast.60, ...), kind=kOutput, calls=%fused_computation.9 | convolution fusion | flops 25755648 | bytes 6606848 | tf_op jit(solution)/shard_map/gjcm,gjcd->gjmd/dot_general | solution.py:113
  176.8 2.1 %convert_reduce_fusion = f32[16,64,512]{2,1,0:T(8,128)} fusion(bf16[4,16,64,512]{3,2,1,0:T(8,128)(2,1)S(1)} %divide_convert_fusion), kind=kLoop, calls=%fused_computation.8 | loop fusion | flops 3670016 | bytes 6291456 | tf_op jit(solution)/shard_map/reduce_sum | solution.py:120
  (57 shorter events, 0.5 us)
Async XLA Ops:
  18.3 10.5 %copy-start.3 = (s32[1024]{0:T(1024)}, s32[1024]{0:T(1024)S(1)}, u32[]{:S(2)}) copy-start(s32[1024]{0:T(1024)S(1)} %pad_clamp_fusion) | copy-start | bytes 12292
  28.2 12.9 %copy-start.2 = (f32[1024]{0:T(1024)S(1)}, f32[1024]{0:T(1024)}, u32[]{:S(2)}) copy-start(f32[1024]{0:T(1024)} %param.8) | copy-start | bytes 12292
  31.5 132.6 %all-to-all-start.1 = ((bf16[4,2,8192]{2,1,0:T(2,128)(2,1)}), bf16[4,2,8192]{2,1,0:T(2,128)(2,1)}, u32[]{:S(2)}, u32[]{:S(2)}) async-start(bf16[4,2,8192]{2,1,0:T(2,128)(2,1)} %reshape.169), calls=%async_computation.1 | async-start | bytes 262144 | tf_op jit(solution)/shard_map/all_to_all | solution.py:97
  36.3 89.4 %all-reduce.3.cloned.1.call-start = ((), (), s32[]{:S(2)}) async-start(), calls=%async_computation.2 | async-start | bytes 262144
  36.6 6.5 %copy-start.5 = (s32[16,2]{1,0:T(8,128)}, s32[16,2]{1,0:T(8,128)S(1)}, u32[]{:S(2)}) copy-start(s32[16,2]{1,0:T(8,128)S(1)} %copy.64) | copy-start | bytes 388
  41.1 6.4 %copy-start.7 = (f32[1024]{0:T(1024)}, f32[1024]{0:T(1024)S(1)}, u32[]{:S(2)}) copy-start(f32[1024]{0:T(1024)S(1)} %add_sqrt_fusion) | copy-start | bytes 12292
  47.5 2.0 %copy-start = (bf16[1024,2048]{1,0:T(8,128)(2,1)}, bf16[1024,2048]{1,0:T(8,128)(2,1)S(1)}, u32[]{:S(2)}) copy-start(bf16[1024,2048]{1,0:T(8,128)(2,1)S(1)} %fusion.1) | copy-start | bytes 12582916
  49.6 17.6 %copy-start.6 = (s32[16,2]{1,0:T(8,128)S(1)}, s32[16,2]{1,0:T(8,128)}, u32[]{:S(2)}) copy-start(s32[16,2]{1,0:T(8,128)} %copy-done.5) | copy-start | bytes 388
  49.6 17.6 %copy-start.11 = (f32[16,64]{1,0:T(8,128)S(1)}, f32[16,64]{1,0:T(8,128)}, u32[]{:S(2)}) copy-start(f32[16,64]{1,0:T(8,128)} %add.124) | copy-start | bytes 12292
  49.6 17.6 %copy-start.12 = (f32[16,2]{1,0:T(8,128)S(1)}, f32[16,2]{1,0:T(8,128)}, u32[]{:S(2)}) copy-start(f32[16,2]{1,0:T(8,128)} %copy.70) | copy-start | bytes 388
  49.6 17.6 %copy-start.13 = (s32[16,2]{1,0:T(8,128)S(1)}, s32[16,2]{1,0:T(8,128)}, u32[]{:S(2)}) copy-start(s32[16,2]{1,0:T(8,128)} %copy.66) | copy-start | bytes 388
  49.6 17.6 %copy-start.14 = (pred[16,2]{1,0:T(8,128)(4,1)S(1)}, pred[16,2]{1,0:T(8,128)(4,1)}, u32[]{:S(2)}) copy-start(pred[16,2]{1,0:T(8,128)(4,1)} %copy.65) | copy-start | bytes 100
  66.5 5.7 %copy-start.1 = (f32[1024,16]{0,1:T(8,128)S(1)}, f32[1024,16]{0,1:T(8,128)}, u32[]{:S(2)}) copy-start(f32[1024,16]{0,1:T(8,128)} %get-tuple-element.21) | copy-start | bytes 196612
  66.9 6.8 %copy-start.8 = (f32[1024]{0:T(1024)S(1)}, f32[1024]{0:T(1024)}, u32[]{:S(2)}) copy-start(f32[1024]{0:T(1024)} %copy-done.7) | copy-start | bytes 12292
  70.2 4.5 %copy-start.15 = (u32[32]{0:T(128)S(1)}, u32[32]{0:T(128)}, u32[]{:S(2)}) copy-start(u32[32]{0:T(128)} %constant.99) | copy-start | bytes 388
  70.2 55.5 %copy-start.9 = (bf16[2,2048]{1,0:T(2,128)(2,1)S(1)}, bf16[2,2048]{1,0:T(2,128)(2,1)}, u32[]{:S(2)}) copy-start(bf16[2,2048]{1,0:T(2,128)(2,1)} %param.5) | copy-start | bytes 24580
  70.2 55.5 %copy-start.10 = (f32[2048]{0:T(1024)S(1)}, f32[2048]{0:T(1024)}, u32[]{:S(2)}) copy-start(f32[2048]{0:T(1024)} %param.9) | copy-start | bytes 24580
  70.2 65.5 %copy-start.4 = (s32[1024]{0:T(1024)S(1)}, s32[1024]{0:T(1024)}, u32[]{:S(2)}) copy-start(s32[1024]{0:T(1024)} %copy-done.3) | copy-start | bytes 12292
  140.1 19.2 %collective-permute-start = (bf16[1,16,2,64]{3,2,1,0:T(2,128)(2,1)S(1)}, bf16[1,16,2,64]{3,2,1,0:T(2,128)(2,1)S(1)}, u32[]{:S(2)}, u32[]{:S(2)}) collective-permute-start(bf16[1,16,2,64]{3,2,1,0:T(2,128)(2,1)S(1)} %bitcast.61), channel_id=1, source_target_pairs={{0,24},{8,0},{16,8},{24,16},{1,25},{9,1},{17,9},{25,17},{2,26},{10... | collective-permute-start | bytes 12296 | tf_op jit(solution)/shard_map/ppermute | solution.py:19
  159.3 4.7 %collective-permute-start.1 = (bf16[2,16,2,64]{3,2,1,0:T(2,128)(2,1)S(1)}, bf16[2,16,2,64]{3,2,1,0:T(2,128)(2,1)S(1)}, u32[]{:S(2)}, u32[]{:S(2)}) collective-permute-start(bf16[2,16,2,64]{3,2,1,0:T(2,128)(2,1)S(1)} %pad_maximum_fusion), channel_id=1, source_target_pairs={{0,16},{8,24},{16,0},{24,8},{1,17},{9,25},{17,1},{25,9},{2,18},{10... | collective-permute-start | bytes 24584 | tf_op jit(solution)/shard_map/ppermute | solution.py:19
  164.1 9.2 %all-to-all-start = ((bf16[4,2,8192]{2,1,0:T(2,128)(2,1)}), bf16[4,2,8192]{2,1,0:T(2,128)(2,1)S(1)}, u32[]{:S(2)}, u32[]{:S(2)}) async-start(bf16[4,2,8192]{2,1,0:T(2,128)(2,1)} %reshape.171), calls=%async_computation | async-start | bytes 262144 | tf_op jit(solution)/shard_map/all_to_all | solution.py:98
Sparse Core Ops, SparseCore 0:
  72.3 53.3 all-reduce.2
